TPU v7x, 32 devices: a whole 2x2x4 slice. The times are simulated.
32 devices in a mesh: dp: 16 (over z, y, core), mp: 2 (over x).
Axes of the slice: x: 2, y: 2, z: 4, core: 2. Of those that a mesh axis runs over, the one named last changes fastest.
Arguments:
- hidden_in: bfloat16 [8192, 4096], P('dp'), may hold values from -1.5 to 1.5
- w_query: bfloat16 [4096, 4096], P('dp', 'mp'), may hold values from -1 to 1
- w_key: bfloat16 [4096, 1024], P('dp', 'mp'), may hold values from -24 to 24
- w_value: bfloat16 [4096, 1024], P('dp', 'mp'), may hold values from -1 to 1
- w_out: bfloat16 [4096, 4096], P('dp', 'mp'), may hold values from -1 to 1
- value_weight: float32 [4096], P('mp'), may hold values from -0.09375 to 0.09375
- rewards: float32 [8192], P('dp'), may hold values from -0.6 to 0.6
- old_values: float32 [8192], P('dp'), may hold values from -6 to 6
- lengths: int32 [64], replicated, may hold values from 1 to 2048, 8192 in all
- terminal: int32 [64], replicated, may hold values 0 or 1
Outputs:
- value: float32 [8192], P('dp')
- advantage: float32 [8192], P('dp')
- value_loss: float32 [], replicated
All inputs are finite; a program needn't handle non-finite values.
Results may differ from a plain program's by a relative error of at most 0.012.
The roundings to bfloat16 on the way count: a program that leaves them out, or rounds other values in their place, can miss the bound.
Values may be sent and summed in bfloat16 or wider, within the bound.
No kernel may reach another device: no remote copies, remote signals or barrier semaphores. Data moves between devices by JAX's collectives and lax.ppermute only.
A program may use at most 128 MiB of HBM per device.

v0:
```python
import jax
import jax.numpy as jnp
from jax import lax
from jax.sharding import PartitionSpec as P

HEAD = 128
discount = 0.999
trace_decay = 0.997
clip_range = 0.2
epsilon = 1e-05
rope_base = 500000.0


def from_behind(array, axis, by):
    size = lax.axis_size(axis)
    pairs = [(i, i + by) for i in range(size) if 0 <= i + by < size]
    return lax.ppermute(array, axis, pairs)


def carried_in(part, axis, combine, identity):
    count = lax.axis_size(axis)
    place = lax.axis_index(axis)
    ahead = count - 1 - place
    gathered = jax.tree.map(lambda a: lax.all_gather(a, axis), part)
    state = jax.tree.map(lambda a, e: jnp.zeros_like(a) + jnp.asarray(e, a.dtype), part, identity)

    def one(hop, state):
        source = count - 1 - hop
        return combine(
            state, jax.tree.map(lambda a: lax.dynamic_index_in_dim(a, source, 0, False), gathered)
        )

    return lax.fori_loop(0, ahead, one, state)


def rotate(states, positions):
    half = HEAD // 2
    freq = rope_base ** (-jnp.arange(half, dtype=jnp.float32) * 2.0 / HEAD)
    angles = positions[:, None] * freq[None, :]
    cosine = jnp.cos(angles)[:, None, :]
    sine = jnp.sin(angles)[:, None, :]
    first = states[..., :half]
    second = states[..., half:]
    return jnp.concatenate([first * cosine - second * sine, second * cosine + first * sine], -1)


def body(
    hidden_in, w_query, w_key, w_value, w_out, value_weight, rewards, old_values, lengths, terminal
):
    rows = hidden_in.shape[0]
    width = hidden_in.shape[1]
    states = hidden_in.astype(jnp.float32)
    normed = (states * lax.rsqrt(jnp.mean(states * states, 1, keepdims=True) + epsilon)).astype(
        jnp.bfloat16
    )
    pieces = (
        lax.all_gather(w_query, "dp", axis=0, tiled=True),
        lax.all_gather(w_key, "dp", axis=0, tiled=True),
        lax.all_gather(w_value, "dp", axis=0, tiled=True),
        lax.all_gather(w_out, "dp", axis=0, tiled=True),
    )
    add_pieces = pieces[:3]
    summed = tuple(
        (jnp.dot(normed, piece, preferred_element_type=jnp.float32) for piece in add_pieces)
    )
    stored = pieces[3]
    query_sum, key_sum, value_sum, whole_out = summed + (stored,)
    position_ids = lax.axis_index("dp") * rows + jnp.arange(rows, dtype=jnp.int32)
    positions = position_ids.astype(jnp.float32)
    local_heads = w_query.shape[1] // HEAD
    local_kv = w_key.shape[1] // HEAD
    group = local_heads // local_kv
    query = rotate(query_sum.reshape(rows, local_heads, HEAD), positions).astype(jnp.bfloat16)
    key = rotate(key_sum.reshape(rows, local_kv, HEAD), positions).astype(jnp.bfloat16)
    values_proj = value_sum.astype(jnp.bfloat16).reshape(rows, local_kv, HEAD)
    ends = jnp.cumsum(lengths)
    matches = ends[None, :] - 1 == position_ids[:, None]
    finished = jnp.any(matches, 1).astype(jnp.float32)
    stopped = jnp.sum(jnp.where(matches, terminal[None, :], 0), 1).astype(jnp.float32)
    episode = jnp.sum((ends[None, :] <= position_ids[:, None]).astype(jnp.int32), 1)
    order = jnp.arange(rows, dtype=jnp.int32)
    same_episode = episode[None, :] == episode[:, None]
    allowed = (order[None, :] <= order[:, None]) & same_episode
    scores = jnp.einsum(
        "tkgd,skd->kgts",
        query.reshape(rows, local_kv, group, HEAD),
        key,
        preferred_element_type=jnp.float32,
    ) * (1.0 / HEAD**0.5)
    masked = jnp.where(allowed[None, None], scores, -1e30)
    largest = jnp.max(masked, -1, keepdims=True)
    expon = jnp.where(allowed[None, None], jnp.exp(masked - largest), 0.0)
    probs = (expon / jnp.sum(expon, -1, keepdims=True)).astype(jnp.bfloat16)
    output = jnp.einsum("kgts,skd->tkgd", probs, values_proj, preferred_element_type=jnp.float32)
    attended = output.astype(jnp.bfloat16).reshape(rows, local_heads * HEAD)
    all_heads = lax.all_gather(attended, "mp", axis=1, tiled=True)
    projected = jnp.dot(all_heads, whole_out, preferred_element_type=jnp.float32)
    feature_count = w_out.shape[1]
    own_states = lax.dynamic_slice_in_dim(
        states, lax.axis_index("mp") * feature_count, feature_count, 1
    )
    residual = own_states + projected
    square_sum, head_sum = lax.psum(
        (jnp.sum(residual * residual, 1), jnp.sum(residual * value_weight[None, :], 1)), "mp"
    )
    value = head_sum * lax.rsqrt(square_sum / width + epsilon)
    following = from_behind(old_values[:1], "dp", -1)
    next_old = jnp.concatenate([old_values[1:], following])
    booted = jnp.where(finished > 0, (1.0 - stopped) * old_values, next_old)
    delta = rewards + discount * booted - old_values
    keep_rate = discount * trace_decay
    spacing = (order[None, :] - order[:, None]).astype(jnp.float32)
    forward_mask = (spacing >= 0.0) & same_episode
    decay_matrix = jnp.where(
        forward_mask, jnp.power(jnp.float32(keep_rate), jnp.maximum(spacing, 0.0)), 0.0
    )
    local_part = jnp.dot(decay_matrix, delta, precision=lax.Precision.HIGHEST)
    remaining = (rows - order).astype(jnp.float32)
    reach = jnp.where(episode == episode[-1], jnp.power(jnp.float32(keep_rate), remaining), 0.0) * (
        1.0 - finished[-1]
    )

    def compose(earlier, later_map):
        return (later_map[0] + later_map[1] * earlier[0], later_map[1] * earlier[1])

    prefix = carried_in(
        (local_part[:1], reach[:1]),
        "dp",
        compose,
        (jnp.zeros((1,), jnp.float32), jnp.ones((1,), jnp.float32)),
    )
    incoming = prefix[0][0]
    advantage = local_part + reach * incoming
    returns = advantage + old_values
    clipped = old_values + jnp.clip(value - old_values, -clip_range, clip_range)
    terms = jnp.maximum((value - returns) ** 2, (clipped - returns) ** 2)
    total_loss = lax.psum(jnp.sum(terms), "dp")
    value_loss = 0.5 * total_loss / (rows * lax.axis_size("dp"))
    return (value, advantage, value_loss)


def solution(mesh):
    return jax.shard_map(
        body,
        mesh=mesh,
        in_specs=(
            P("dp", None),
            P("dp", "mp"),
            P("dp", "mp"),
            P("dp", "mp"),
            P("dp", "mp"),
            P("mp"),
            P("dp"),
            P("dp"),
            P(),
            P(),
        ),
        out_specs=(P("dp"), P("dp"), P()),
        check_vma=False,
    )
```

profile of v0, /device:TPU:0, one launch (start us, length us, event | category | flops | bytes accessed | tf_op | source)
XLA Modules:
  0.0 487.3 jit_solution(12846572343256018310)
XLA Ops:
  7.2 0.7 all-gather.10.cloned.1.call-update
  7.9 0.7 all-gather.8.cloned.1.call-update
  8.7 0.7 all-gather.12.cloned.1.call-update
  10.0 0.7 copy.25
  11.0 0.8 fusion.22
  11.8 3.1 multiply_reduce_fusion
  15.1 1.0 multiply_cosine_fusion
  16.1 47.2 %all-gather.10.cloned.1.call-done = bf16[4096,512]{1,0:T(8,128)(2,1)} async-done(((bf16[256,512]{1,0:T(8,128)(2,1)}), bf16[4096,512]{1,0:T(8,128)(2,1)}) %all-gather.10.cloned.1.call-update) | async-done | bytes 4194320 | tf_op jit(solution)/shard_map/all_gather | solution.py:58
  63.3 5.9 %fusion.32 = f32[512,512]{0,1:T(8,128)S(1)} fusion(bf16[4096,512]{1,0:T(8,128)(2,1)} %all-gather.10.cloned.1.call-done, f32[512]{0:T(512)S(1)} %add_rsqrt_fusion, bf16[512,4096]{1,0:T(8,128)(2,1)} %param.12), kind=kOutput, calls=%fused_computation.70 | convolution fusion | flops 2153775104 | bytes 9439232 | tf_op jit(solution)/shard_map/dot_general | solution.py:64
  69.9 1.1 subtract_convert_fusion.1
  71.0 43.3 %all-gather.8.cloned.1.call-done = bf16[4096,512]{1,0:T(8,128)(2,1)} async-done(((bf16[256,512]{1,0:T(8,128)(2,1)}), bf16[4096,512]{1,0:T(8,128)(2,1)}) %all-gather.8.cloned.1.call-update) | async-done | bytes 4194320 | tf_op jit(solution)/shard_map/all_gather | solution.py:59
  114.4 5.9 %convolution_convert_fusion = bf16[512,512]{0,1:T(8,128)(2,1)S(1)} fusion(bf16[4096,512]{1,0:T(8,128)(2,1)} %all-gather.8.cloned.1.call-done, f32[512]{0:T(512)S(1)} %add_rsqrt_fusion, bf16[512,4096]{1,0:T(8,128)(2,1)} %param.12), kind=kOutput, calls=%fused_computation.26 | convolution fusion | flops 2154037248 | bytes 8914944 | tf_op jit(solution)/shard_map/dot_general | solution.py:64
  120.3 121.2 %all-gather.12.cloned.1.call-done = bf16[4096,2048]{1,0:T(8,128)(2,1)} async-done(((bf16[256,2048]{1,0:T(8,128)(2,1)}), bf16[4096,2048]{1,0:T(8,128)(2,1)}) %all-gather.12.cloned.1.call-update) | async-done | bytes 16777232 | tf_op jit(solution)/shard_map/all_gather | solution.py:57
  241.5 13.2 %convolution_bitcast_fusion = f32[64,8,16,128]{3,1,2,0:T(8,128)S(1)} fusion(bf16[4096,2048]{1,0:T(8,128)(2,1)} %all-gather.12.cloned.1.call-done, f32[512]{0:T(512)S(1)} %add_rsqrt_fusion, bf16[512,4096]{1,0:T(8,128)(2,1)} %param.12), kind=kOutput, calls=%fused_computation.18 | convolution fusion | flops 8596226048 | bytes 25167872 | tf_op jit(solution)/shard_map/dot_general | solution.py:64
  254.8 0.9 copy.36
  255.7 1.8 subtract_convert_fusion
  258.6 8.1 %fusion.6 = f32[4,512,512,4]{2,1,3,0:T(8,128)} fusion(bf16[512,4,4,64]{3,0,2,1:T(8,128)(2,1)S(1)} %bitcast.53, bf16[512,4,4,64]{3,0,2,1:T(8,128)(2,1)S(1)} %bitcast.54, bf16[512,4,64]{2,0,1:T(8,128)(2,1)S(1)} %copy-done, bf16[512,4,64]{2,0,1:T(8,128)(2,1)S(1)} %get-tuple-element.113), kind=kOutput, calls=%fused_computation.19 | convolution fusion | flops 1078984704 | bytes 19398656 | tf_op jit(solution)/shard_map/tkgd,skd->kgts/dot_general | solution.py:84
  266.8 17.9 %fusion.34 = (f32[4,4,512]{2,1,0:T(4,128)S(1)}, f32[4,4,512,512]{2,3,1,0:T(8,128)}) fusion(f32[4,512,512,4]{2,1,3,0:T(8,128)} %fusion.6, pred[512,512]{0,1:T(8,128)(4,1)S(1)} %compare_and_fusion.1), kind=kOutput, calls=%fused_computation.72 | output fusion | flops 29360640 | bytes 33849344 | tf_op jit(solution)/shard_map/sub | solution.py:92
  284.7 8.6 %fusion.10 = bf16[4,128,4,512]{3,1,2,0:T(8,128)(2,1)} fusion(bf16[512,4,128,1]{0,2,3,1:T(8,128)(2,1)S(1)} %bitcast.63, f32[4,4,512,512]{2,3,1,0:T(8,128)} %get-tuple-element.120, f32[4,4,512]{2,1,0:T(4,128)S(1)} %get-tuple-element.119), kind=kOutput, calls=%fused_computation.23 | convolution fusion | flops 1083179008 | bytes 19431424 | tf_op jit(solution)/shard_map/kgts,skd->tkgd/dot_general | solution.py:94
  293.9 1.3 collective-permute-start
  295.2 6.5 %convert_element_type.45 = f32[512,4096]{1,0:T(8,128)} convert(bf16[512,4096]{1,0:T(8,128)(2,1)} %param.12) | non-fusion elementwise | flops 2097152 | bytes 12582912 | tf_op jit(solution)/shard_map/convert_element_type | solution.py:52
  301.7 0.6 slice.36
  303.8 0.6 dynamic-slice
  304.4 0.7 select_multiply_fusion
  305.1 0.7 slice_dynamic-update-slice_fusion
  305.8 0.7 fusion.25
  306.5 1.1 fusion.11
  307.6 0.7 slice_dynamic-update-slice_fusion.1
  308.3 34.8 %all-reduce.2 = (f32[16]{0:T(128)S(1)}, f32[16]{0:T(128)S(1)}) all-reduce(f32[16]{0:T(128)S(1)} %slice_dynamic-update-slice_fusion.1, f32[16]{0:T(128)S(1)} %slice_dynamic-update-slice_fusion), channel_id=2, replica_groups=mesh['dp'=16,'mp'=2] {'dp'}, use_global_device_ids=true, to_apply=%add | all-reduce | flops 32 | bytes 256
  343.1 28.6 %while.14 = (s32[]{:T(128)}, f32[1]{0:T(128)}, s32[]{:T(128)}, f32[16,1]{0,1:T(1,128)S(1)}, f32[16,1]{0,1:T(1,128)S(1)}, /*index=5*/s32[]{:T(128)}, s32[]{:T(128)}, s32[]{:T(128)}, s32[]{:T(128)}) while((s32[]{:T(128)}, f32[1]{0:T(128)}, s32[]{:T(128)}, f32[16,1]{0,1:T(1,128)S(1)}, f32[16,1]{0,1:T(1,128)S(1)}, /*index=5*/s32[]{:T(128)}, ...), condition=%wide.region_12.13_spmd, body=%wide.region_11.12_spmd.sunk | while | flops 8 | bytes 183 | solution.py:33
  343.1 0.6 constant_dynamic-slice_fusion.3
  345.0 0.6 constant_dynamic-slice_fusion.3
  346.9 0.6 constant_dynamic-slice_fusion.3
  348.9 0.6 constant_dynamic-slice_fusion.3
  350.8 0.6 constant_dynamic-slice_fusion.3
  352.7 0.6 constant_dynamic-slice_fusion.3
  354.6 0.6 constant_dynamic-slice_fusion.3
  356.5 0.6 constant_dynamic-slice_fusion.3
  358.4 0.6 constant_dynamic-slice_fusion.3
  360.3 0.6 constant_dynamic-slice_fusion.3
  362.2 0.6 constant_dynamic-slice_fusion.3
  366.0 0.6 constant_dynamic-slice_fusion.3
  369.8 0.6 constant_dynamic-slice_fusion.3
  371.7 53.4 %all-gather.14.cloned.1.call-done = bf16[512,4096]{0,1:T(8,128)(2,1)} async-done(((bf16[512,2048]{0,1:T(8,128)(2,1)}), bf16[512,4096]{0,1:T(8,128)(2,1)}) %all-gather.14.cloned.1.call-update) | async-done | bytes 4194320 | tf_op jit(solution)/shard_map/all_gather | solution.py:96
  425.1 14.6 %multiply_reduce_fusion.1 = (f32[512]{0:T(512)S(1)}, f32[512]{0:T(512)S(1)}) fusion(f32[2048]{0:T(1024)S(1)} %copy-done.3, bf16[512,4096]{0,1:T(8,128)(2,1)} %all-gather.14.cloned.1.call-done, bf16[4096,2048]{1,0:T(8,128)(2,1)} %all-gather.16.cloned.1.call-done, f32[512,4096]{1,0:T(8,128)} %convert_element_type.45, s32[]{:T(128)S(6)} %select_n.35), kind=kOutput, calls=%fused_computation.13 | convolution fusion | flops 8595177472 | bytes 25178116 | tf_op jit(solution)/shard_map/dot_general | solution.py:97
  439.7 4.9 %all-reduce.3 = (f32[512]{0:T(512)S(1)}, f32[512]{0:T(512)S(1)}) all-reduce(f32[512]{0:T(512)S(1)} %get-tuple-element.89, f32[512]{0:T(512)S(1)} %get-tuple-element.88), channel_id=1, replica_groups=mesh['dp'=16,'mp'=2] {'mp'}, use_global_device_ids=true, to_apply=%region_6.7 | all-reduce | flops 1024 | bytes 8192 | tf_op jit(solution)/shard_map/psum | solution.py:103
  444.7 1.9 maximum_reduce_fusion
  446.5 32.5 %psum.23 = f32[]{:T(128)} all-reduce(f32[]{:T(128)} %get-tuple-element.106), channel_id=1, replica_groups=mesh['dp'=16,'mp'=2] {'dp'}, use_global_device_ids=true, to_apply=%region_14.15 | all-reduce | flops 1 | bytes 8 | tf_op jit(solution)/shard_map/psum | solution.py:137
  (41 shorter events, 5.6 us)
Async XLA Ops:
  7.2 56.1 %all-gather.10.cloned.1.call-start = ((), (), s32[]{:S(2)}) async-start(), calls=%async_computation.1 | async-start | bytes 4456448 | tf_op jit(solution)/shard_map/all_gather | solution.py:58
  7.9 106.5 %all-gather.8.cloned.1.call-start = ((), (), s32[]{:S(2)}) async-start(), calls=%async_computation | async-start | bytes 4456448 | tf_op jit(solution)/shard_map/all_gather | solution.py:59
  8.7 232.9 %all-gather.12.cloned.1.call-start = ((), (), s32[]{:S(2)}) async-start(), calls=%async_computation.2 | async-start | bytes 17825792 | tf_op jit(solution)/shard_map/all_gather | solution.py:57
  9.4 362.3 %all-gather.16.cloned.1.call-start = ((), (), s32[]{:S(2)}) async-start(), calls=%async_computation.4 | async-start | bytes 17825792 | tf_op jit(solution)/shard_map/all_gather | solution.py:60
  10.0 415.2 %all-gather.14.cloned.1.call-start = ((), (), s32[]{:S(2)}) async-start(), calls=%async_computation.3 | async-start | bytes 6291456 | tf_op jit(solution)/shard_map/all_gather | solution.py:96
  257.5 1.1 copy-start
  284.7 8.6 %copy-start.1 = (f32[512]{0:T(512)S(1)}, f32[512]{0:T(512)}, u32[]{:S(2)}) copy-start(f32[512]{0:T(512)} %param.19) | copy-start | bytes 6148
  293.9 12.0 %collective-permute-start = (f32[1]{0:T(128)}, f32[1]{0:T(128)}, u32[]{:S(2)}, u32[]{:S(2)}) collective-permute-start(f32[1]{0:T(128)} %slice.35), channel_id=1, source_target_pairs={{2,0},{4,2},{6,4},{8,6},{10,8},{12,10},{14,12},{16,14},{18,16},{20... | collective-permute-start | bytes 20 | tf_op jit(solution)/shard_map/ppermute | solution.py:17
  295.2 8.6 %copy-start.4 = (u32[32]{0:T(128)S(1)}, u32[32]{0:T(128)}, u32[]{:S(2)}) copy-start(u32[32]{0:T(128)} %constant.106) | copy-start | bytes 388
  295.2 10.7 %copy-start.2 = (f32[512]{0:T(512)S(1)}, f32[512]{0:T(512)}, u32[]{:S(2)}) copy-start(f32[512]{0:T(512)} %param.18) | copy-start | bytes 6148
  295.2 130.0 %copy-start.3 = (f32[2048]{0:T(1024)S(1)}, f32[2048]{0:T(1024)}, u32[]{:S(2)}) copy-start(f32[2048]{0:T(1024)} %param.17) | copy-start | bytes 24580
Sparse Core Ops, SparseCore 0:
  10.1 53.0 all-gather.9
  65.4 48.8 all-gather.7
  116.5 124.9 all-gather.11
  243.6 125.2 all-gather.15
  370.2 54.8 all-gather.13
where the time goes:
time: 488 us; the launch traced here: 487 us
  waiting for transfers between devices  268 us (55%)
  blocking collectives  72.2 us (15%)
  matrix products  57.5 us (12%)
  other arithmetic  36 us (7%)
  loops' own time  19.3 us (4%)
  local copies, waits for them, and re-layouts  16.7 us (3%)
  between operations  16.4 us (3%)
    all_gather x1, waiting for transfers between devices, body(): lax.all_gather(w_query, 'dp', axis=0, tiled=True)  121 us
    all_gather x1, waiting for transfers between devices, body(): all_heads = lax.all_gather(attended, 'mp', axis=1, tiled=True)  53.4 us
    all_gather x1, waiting for transfers between devices, body(): lax.all_gather(w_key, 'dp', axis=0, tiled=True)  47.2 us
    all_gather x1, waiting for transfers between devices, body(): lax.all_gather(w_value, 'dp', axis=0, tiled=True)  43.3 us
    unnamed x1, blocking collectives  34.8 us
    psum x1, blocking collectives, body(): total_loss = lax.psum(jnp.sum(terms), 'dp')  32.5 us
    dot_general x3, matrix products, body(): jnp.dot(normed, piece, preferred_element_type=jnp.float32)  25 us
    another operation x1, loops' own time, carried_in(): return lax.fori_loop(0, ahead, one, state)  19.3 us
  transfers between devices with their start and end apart: 6, of which 4 were waited for; matrix products, arithmetic and copies ran while one was open for 19% of the time, Pallas kernels for 0%

commit v1 on v0

--- a/solution.py
+++ b/solution.py
@@ -9,6 +9,24 @@
 clip_range = 0.2
 epsilon = 1e-05
 rope_base = 500000.0
+
+
+def ring_gather(value, axis, dim):
+    ways, here, hop = (lax.axis_size(axis), lax.axis_index(axis), value.shape[dim])
+    shape = [n * ways if d == dim else n for d, n in enumerate(value.shape)]
+    full = lax.dynamic_update_slice_in_dim(
+        jnp.zeros(shape, value.dtype), value, here * hop, axis=dim
+    )
+    going_up = going_down = value
+    for far in range(1, ways // 2 + 1):
+        going_up = lax.ppermute(going_up, axis, [(d, (d + 1) % ways) for d in range(ways)])
+        full = lax.dynamic_update_slice_in_dim(full, going_up, (here - far) % ways * hop, axis=dim)
+        if 2 * far < ways:
+            going_down = lax.ppermute(going_down, axis, [(d, (d - 1) % ways) for d in range(ways)])
+            full = lax.dynamic_update_slice_in_dim(
+                full, going_down, (here + far) % ways * hop, axis=dim
+            )
+    return full
 
 
 def from_behind(array, axis, by):
@@ -56,7 +74,7 @@
     pieces = (
         lax.all_gather(w_query, "dp", axis=0, tiled=True),
         lax.all_gather(w_key, "dp", axis=0, tiled=True),
-        lax.all_gather(w_value, "dp", axis=0, tiled=True),
+        ring_gather(w_value, "dp", 0),
         lax.all_gather(w_out, "dp", axis=0, tiled=True),
     )
     add_pieces = pieces[:3]

time: 488 us -> 454 us (0.930)
  waiting for transfers between devices: 268 us -> 189 us
  starting transfers between devices: 1.47 us -> 35.3 us
  local copies, waits for them, and re-layouts: 16.7 us -> 29.4 us
    all_gather x1, waiting for transfers between devices: 47.2 us -> 0.01 us  [body(): lax.all_gather(w_key, 'dp', axis=0, tiled=True)]
    all_gather x1 -> x0, waiting for transfers between devices: 43.3 us -> none  [body(): lax.all_gather(w_value, 'dp', axis=0, tiled=True)]
    ppermute x0 -> x15, starting transfers between devices: none -> 33.9 us  [the longest x7 32.2 us: ring_gather(): lax.ppermute(going_down, axis, [(d, (d - 1) % ways) for d in range(ways)])]
    ppermute x0 -> x15, waiting for transfers between devices: none -> 26.9 us  [the longest x8 21.8 us: ring_gather(): lax.ppermute(going_up, axis, [(d, (d + 1) % ways) for d in range(ways)])]
    all_gather x1, waiting for transfers between devices: 121 us -> 104 us  [body(): lax.all_gather(w_query, 'dp', axis=0, tiled=True)]
    dynamic_update_slice x0 -> x16, local copies, waits for them, and re-layouts: none -> 11.5 us  [the longest x8 5.76 us: ring_gather(): lax.dynamic_update_slice_in_dim(full, going_up, (here - far) % ways * hop...]
  transfers between devices with their start and end apart: 6 -> 20, of which waited for: 4 -> 11; matrix products, arithmetic and copies ran while one was open for 19% -> 23% of each run, Pallas kernels for 0% -> 0%
where the time goes in v1:
time: 454 us; the launch traced here: 453 us
  waiting for transfers between devices  189 us (42%)
  blocking collectives  72.1 us (16%)
  matrix products  57.5 us (13%)
  starting transfers between devices  35.3 us (8%)
  other arithmetic  35 us (8%)
  local copies, waits for them, and re-layouts  29.4 us (6%)
  loops' own time  18.3 us (4%)
  between operations  16.5 us (4%)
    all_gather x1, waiting for transfers between devices, body(): lax.all_gather(w_query, 'dp', axis=0, tiled=True)  104 us
    all_gather x1, waiting for transfers between devices, body(): all_heads = lax.all_gather(attended, 'mp', axis=1, tiled=True)  55.4 us
    unnamed x1, blocking collectives  34.7 us
    psum x1, blocking collectives, body(): total_loss = lax.psum(jnp.sum(terms), 'dp')  32.5 us
    ppermute x7, starting transfers between devices, ring_gather(): lax.ppermute(going_down, axis, [(d, (d - 1) % ways) for d in range(ways)])  32.2 us
    dot_general x3, matrix products, body(): jnp.dot(normed, piece, preferred_element_type=jnp.float32)  25.1 us
    ppermute x8, waiting for transfers between devices, ring_gather(): lax.ppermute(going_up, axis, [(d, (d + 1) % ways) for d in range(ways)])  21.8 us
    another operation x1, loops' own time, carried_in(): return lax.fori_loop(0, ahead, one, state)  18.3 us
  transfers between devices with their start and end apart: 20, of which 11 were waited for; matrix products, arithmetic and copies ran while one was open for 23% of the time, Pallas kernels for 0%

profile of v1, /device:TPU:0, one launch (start us, length us, event | category | flops | bytes accessed | tf_op | source)
XLA Modules:
  0.0 453.0 jit_solution(18310665345968425301)
XLA Ops:
  10.0 5.0 %collective-permute-start.1 = (bf16[256,512]{1,0:T(8,128)(2,1)}, bf16[256,512]{1,0:T(8,128)(2,1)S(1)}, u32[]{:S(2)}, u32[]{:S(2)}) collective-permute-start(bf16[256,512]{1,0:T(8,128)(2,1)} %param.15), channel_id=1, source_target_pairs={{0,30},{2,0},{4,2},{6,4},{8,6},{10,8},{12,10},{14,12},{16,14},{18,... | collective-permute-start | bytes 786440 | tf_op jit(solution)/shard_map/ppermute | solution.py:25
  15.1 3.1 multiply_reduce_fusion
  18.5 1.0 multiply_cosine_fusion
  19.6 4.5 collective-permute-start.3
  24.2 6.9 %collective-permute-done.2 = bf16[256,512]{1,0:T(8,128)(2,1)S(1)} collective-permute-done((bf16[256,512]{1,0:T(8,128)(2,1)S(1)}, bf16[256,512]{1,0:T(8,128)(2,1)S(1)}, u32[]{:S(2)}, u32[]{:S(2)}) %collective-permute-start.2) | collective-permute-done | bytes 262176 | tf_op jit(solution)/shard_map/ppermute | solution.py:22
  31.4 4.5 collective-permute-start.5
  35.8 3.9 collective-permute-done.4
  39.8 2.2 broadcast_in_dim.30
  42.0 0.7 constant_dynamic-update-slice_fusion.15
  42.8 0.7 constant_dynamic-update-slice_fusion.14
  43.5 4.4 collective-permute-start.7
  48.6 1.9 collective-permute-done.6
  51.3 0.7 constant_dynamic-update-slice_fusion.11
  52.1 4.7 %collective-permute-start.9 = (bf16[256,512]{1,0:T(8,128)(2,1)S(1)}, bf16[256,512]{1,0:T(8,128)(2,1)S(1)}, u32[]{:S(2)}, u32[]{:S(2)}) collective-permute-start(bf16[256,512]{1,0:T(8,128)(2,1)S(1)} %collective-permute-done.7), channel_id=1, source_target_pairs={{0,30},{2,0},{4,2},{6,4},{8,6},{10,8},{12,10},{14,12},{16,14},{18,... | collective-permute-start | bytes 786440 | tf_op jit(solution)/shard_map/ppermute | solution.py:25
  57.5 2.3 collective-permute-done.8
  59.8 0.7 constant_dynamic-update-slice_fusion.9
  60.5 0.7 constant_dynamic-update-slice_fusion.8
  61.2 4.4 collective-permute-start.11
  66.4 2.0 collective-permute-done.10
  68.4 1.1 collective-permute-start.12
  71.0 3.3 collective-permute-done.11
  74.3 4.6 %collective-permute-start.13 = (bf16[256,512]{1,0:T(8,128)(2,1)S(1)}, bf16[256,512]{1,0:T(8,128)(2,1)S(1)}, u32[]{:S(2)}, u32[]{:S(2)}) collective-permute-start(bf16[256,512]{1,0:T(8,128)(2,1)S(1)} %collective-permute-done.11), channel_id=1, source_target_pairs={{0,30},{2,0},{4,2},{6,4},{8,6},{10,8},{12,10},{14,12},{16,14},{18,... | collective-permute-start | bytes 786440 | tf_op jit(solution)/shard_map/ppermute | solution.py:25
  80.3 0.7 constant_dynamic-update-slice_fusion.2
  81.1 1.7 collective-permute-done.13
  83.5 4.6 %collective-permute-done.14 = bf16[256,512]{1,0:T(8,128)(2,1)S(1)} collective-permute-done((bf16[256,512]{1,0:T(8,128)(2,1)S(1)}, bf16[256,512]{1,0:T(8,128)(2,1)S(1)}, u32[]{:S(2)}, u32[]{:S(2)}) %collective-permute-start.14) | collective-permute-done | bytes 262176 | tf_op jit(solution)/shard_map/ppermute | solution.py:22
  88.1 0.7 constant_dynamic-update-slice_fusion
  88.9 5.9 %convolution_convert_fusion = bf16[512,512]{0,1:T(8,128)(2,1)} fusion(bf16[4096,512]{1,0:T(8,128)(2,1)} %constant_dynamic-update-slice_fusion, f32[512]{0:T(512)S(1)} %add_rsqrt_fusion, bf16[512,4096]{1,0:T(8,128)(2,1)S(1)} %copy-done), kind=kOutput, calls=%fused_computation.26 | convolution fusion | flops 2154037248 | bytes 8914944 | tf_op jit(solution)/shard_map/dot_general | solution.py:82
  94.8 5.9 %fusion.32 = f32[512,512]{0,1:T(8,128)S(1)} fusion(bf16[4096,512]{1,0:T(8,128)(2,1)} %all-gather.7.cloned.1.call-done, f32[512]{0:T(512)S(1)} %add_rsqrt_fusion, bf16[512,4096]{1,0:T(8,128)(2,1)} %param.12), kind=kOutput, calls=%fused_computation.86 | convolution fusion | flops 2153775104 | bytes 9439232 | tf_op jit(solution)/shard_map/dot_general | solution.py:82
  101.5 1.1 subtract_convert_fusion.1
  102.6 104.5 %all-gather.9.cloned.1.call-done = bf16[4096,2048]{1,0:T(8,128)(2,1)} async-done(((bf16[256,2048]{1,0:T(8,128)(2,1)}), bf16[4096,2048]{1,0:T(8,128)(2,1)}) %all-gather.9.cloned.1.call-update) | async-done | bytes 16777232 | tf_op jit(solution)/shard_map/all_gather | solution.py:75
  207.1 13.2 %convolution_bitcast_fusion = f32[64,8,16,128]{3,1,2,0:T(8,128)S(1)} fusion(bf16[4096,2048]{1,0:T(8,128)(2,1)} %all-gather.9.cloned.1.call-done, f32[512]{0:T(512)S(1)} %add_rsqrt_fusion, bf16[512,4096]{1,0:T(8,128)(2,1)} %param.12), kind=kOutput, calls=%fused_computation.18 | convolution fusion | flops 8596226048 | bytes 25167872 | tf_op jit(solution)/shard_map/dot_general | solution.py:82
  220.3 0.9 copy.36
  221.2 1.6 subtract_convert_fusion
  223.9 8.2 %fusion.6 = f32[4,512,512,4]{2,1,3,0:T(8,128)} fusion(bf16[512,4,4,64]{3,0,2,1:T(8,128)(2,1)S(1)} %bitcast.53, bf16[512,4,4,64]{3,0,2,1:T(8,128)(2,1)S(1)} %bitcast.54, bf16[512,4,64]{2,0,1:T(8,128)(2,1)S(1)} %copy-done.1, bf16[512,4,64]{2,0,1:T(8,128)(2,1)S(1)} %get-tuple-element.113), kind=kOutput, calls=%fused_computation.19 | convolution fusion | flops 1078984704 | bytes 19398656 | tf_op jit(solution)/shard_map/tkgd,skd->kgts/dot_general | solution.py:102
  232.1 18.0 %fusion.34 = (f32[4,4,512]{2,1,0:T(4,128)S(1)}, f32[4,4,512,512]{2,3,1,0:T(8,128)}) fusion(f32[4,512,512,4]{2,1,3,0:T(8,128)} %fusion.6, pred[512,512]{0,1:T(8,128)(4,1)S(1)} %compare_and_fusion.1), kind=kOutput, calls=%fused_computation.88 | output fusion | flops 29360640 | bytes 33849344 | tf_op jit(solution)/shard_map/sub | solution.py:110
  250.1 8.6 %fusion.10 = bf16[4,128,4,512]{3,1,2,0:T(8,128)(2,1)} fusion(bf16[512,4,128,1]{0,2,3,1:T(8,128)(2,1)S(1)} %bitcast.63, f32[4,4,512,512]{2,3,1,0:T(8,128)} %get-tuple-element.120, f32[4,4,512]{2,1,0:T(4,128)S(1)} %get-tuple-element.119), kind=kOutput, calls=%fused_computation.23 | convolution fusion | flops 1083179008 | bytes 19431424 | tf_op jit(solution)/shard_map/kgts,skd->tkgd/dot_general | solution.py:112
  259.2 1.3 collective-permute-start.15
  261.2 6.5 %convert_element_type.45 = f32[512,4096]{1,0:T(8,128)} convert(bf16[512,4096]{1,0:T(8,128)(2,1)} %param.12) | non-fusion elementwise | flops 2097152 | bytes 12582912 | tf_op jit(solution)/shard_map/convert_element_type | solution.py:70
  270.4 0.7 slice_dynamic-update-slice_fusion
  271.8 1.1 fusion.11
  272.9 0.7 slice_dynamic-update-slice_fusion.1
  273.6 34.7 %all-reduce.2 = (f32[16]{0:T(128)S(1)}, f32[16]{0:T(128)S(1)}) all-reduce(f32[16]{0:T(128)S(1)} %slice_dynamic-update-slice_fusion.1, f32[16]{0:T(128)S(1)} %slice_dynamic-update-slice_fusion), channel_id=2, replica_groups=mesh['dp'=16,'mp'=2] {'dp'}, use_global_device_ids=true, to_apply=%add | all-reduce | flops 32 | bytes 256
  308.3 27.1 %while.14 = (s32[]{:T(128)}, f32[1]{0:T(128)}, s32[]{:T(128)}, f32[16,1]{0,1:T(1,128)S(1)}, f32[16,1]{0,1:T(1,128)S(1)}, /*index=5*/s32[]{:T(128)}, s32[]{:T(128)}, s32[]{:T(128)}, s32[]{:T(128)}) while((s32[]{:T(128)}, f32[1]{0:T(128)}, s32[]{:T(128)}, f32[16,1]{0,1:T(1,128)S(1)}, f32[16,1]{0,1:T(1,128)S(1)}, /*index=5*/s32[]{:T(128)}, ...), condition=%wide.region_12.13_spmd, body=%wide.region_11.12_spmd.sunk | while | flops 8 | bytes 191 | solution.py:51
  335.4 55.4 %all-gather.11.cloned.1.call-done = bf16[512,4096]{0,1:T(8,128)(2,1)} async-done(((bf16[512,2048]{0,1:T(8,128)(2,1)}), bf16[512,4096]{0,1:T(8,128)(2,1)}) %all-gather.11.cloned.1.call-update) | async-done | bytes 4194320 | tf_op jit(solution)/shard_map/all_gather | solution.py:114
  390.9 14.6 %multiply_reduce_fusion.1 = (f32[512]{0:T(512)S(1)}, f32[512]{0:T(512)S(1)}) fusion(f32[2048]{0:T(1024)S(1)} %copy-done.7, bf16[512,4096]{0,1:T(8,128)(2,1)} %all-gather.11.cloned.1.call-done, bf16[4096,2048]{1,0:T(8,128)(2,1)} %all-gather.13.cloned.1.call-done, f32[512,4096]{1,0:T(8,128)} %convert_element_type.45, s32[]{:T(128)S(6)} %select_n.146), kind=kOutput, calls=%fused_computation.13 | convolution fusion | flops 8595177472 | bytes 25178116 | tf_op jit(solution)/shard_map/dot_general | solution.py:115
  405.5 4.9 %all-reduce.3 = (f32[512]{0:T(512)S(1)}, f32[512]{0:T(512)S(1)}) all-reduce(f32[512]{0:T(512)S(1)} %get-tuple-element.89, f32[512]{0:T(512)S(1)} %get-tuple-element.88), channel_id=1, replica_groups=mesh['dp'=16,'mp'=2] {'mp'}, use_global_device_ids=true, to_apply=%region_6.7 | all-reduce | flops 1024 | bytes 8192 | tf_op jit(solution)/shard_map/psum | solution.py:121
  410.4 1.8 maximum_reduce_fusion
  412.2 32.5 %psum.23 = f32[]{:T(128)} all-reduce(f32[]{:T(128)} %get-tuple-element.106), channel_id=1, replica_groups=mesh['dp'=16,'mp'=2] {'dp'}, use_global_device_ids=true, to_apply=%region_14.15 | all-reduce | flops 1 | bytes 8 | tf_op jit(solution)/shard_map/psum | solution.py:155
  (95 shorter events, 24.5 us)
Async XLA Ops:
  7.2 11.0 %copy-start.5 = (s32[64]{0:T(128)S(1)}, s32[64]{0:T(128)}, u32[]{:S(2)}) copy-start(s32[64]{0:T(128)} %param.20) | copy-start | bytes 772
  7.2 16.9 %copy-start.6 = (s32[64]{0:T(128)S(1)}, s32[64]{0:T(128)}, u32[]{:S(2)}) copy-start(s32[64]{0:T(128)} %param.21) | copy-start | bytes 772
  7.2 87.6 %all-gather.7.cloned.1.call-start = ((), (), s32[]{:S(2)}) async-start(), calls=%async_computation | async-start | bytes 4456448 | tf_op jit(solution)/shard_map/all_gather | solution.py:76
  7.9 199.2 %all-gather.9.cloned.1.call-start = ((), (), s32[]{:S(2)}) async-start(), calls=%async_computation.1 | async-start | bytes 17825792 | tf_op jit(solution)/shard_map/all_gather | solution.py:75
  8.7 326.8 %all-gather.13.cloned.1.call-start = ((), (), s32[]{:S(2)}) async-start(), calls=%async_computation.3 | async-start | bytes 17825792 | tf_op jit(solution)/shard_map/all_gather | solution.py:78
  9.4 381.5 %all-gather.11.cloned.1.call-start = ((), (), s32[]{:S(2)}) async-start(), calls=%async_computation.2 | async-start | bytes 6291456 | tf_op jit(solution)/shard_map/all_gather | solution.py:114
  9.5 10.0 %collective-permute-start = (bf16[256,512]{1,0:T(8,128)(2,1)}, bf16[256,512]{1,0:T(8,128)(2,1)S(1)}, u32[]{:S(2)}, u32[]{:S(2)}) collective-permute-start(bf16[256,512]{1,0:T(8,128)(2,1)} %param.15), channel_id=1, source_target_pairs={{0,2},{2,4},{4,6},{6,8},{8,10},{10,12},{12,14},{14,16},{16,18},{18... | collective-permute-start | bytes 786440 | tf_op jit(solution)/shard_map/ppermute | solution.py:22
  10.0 9.6 %collective-permute-start.1 = (bf16[256,512]{1,0:T(8,128)(2,1)}, bf16[256,512]{1,0:T(8,128)(2,1)S(1)}, u32[]{:S(2)}, u32[]{:S(2)}) collective-permute-start(bf16[256,512]{1,0:T(8,128)(2,1)} %param.15), channel_id=1, source_target_pairs={{0,30},{2,0},{4,2},{6,4},{8,6},{10,8},{12,10},{14,12},{16,14},{18,... | collective-permute-start | bytes 786440 | tf_op jit(solution)/shard_map/ppermute | solution.py:25
  15.1 27.0 %copy-start.2 = (bf16[256,512]{1,0:T(8,128)(2,1)S(1)}, bf16[256,512]{1,0:T(8,128)(2,1)}, u32[]{:S(2)}) copy-start(bf16[256,512]{1,0:T(8,128)(2,1)} %param.15) | copy-start | bytes 786436
  19.5 11.6 %collective-permute-start.2 = (bf16[256,512]{1,0:T(8,128)(2,1)S(1)}, bf16[256,512]{1,0:T(8,128)(2,1)S(1)}, u32[]{:S(2)}, u32[]{:S(2)}) collective-permute-start(bf16[256,512]{1,0:T(8,128)(2,1)S(1)} %collective-permute-done), channel_id=1, source_target_pairs={{0,2},{2,4},{4,6},{6,8},{8,10},{10,12},{12,14},{14,16},{16,18},{18... | collective-permute-start | bytes 786440 | tf_op jit(solution)/shard_map/ppermute | solution.py:22
  19.6 11.7 %collective-permute-start.3 = (bf16[256,512]{1,0:T(8,128)(2,1)S(1)}, bf16[256,512]{1,0:T(8,128)(2,1)S(1)}, u32[]{:S(2)}, u32[]{:S(2)}) collective-permute-start(bf16[256,512]{1,0:T(8,128)(2,1)S(1)} %collective-permute-done.1), channel_id=1, source_target_pairs={{0,30},{2,0},{4,2},{6,4},{8,6},{10,8},{12,10},{14,12},{16,14},{18,... | collective-permute-start | bytes 786440 | tf_op jit(solution)/shard_map/ppermute | solution.py:25
  31.1 8.7 %collective-permute-start.4 = (bf16[256,512]{1,0:T(8,128)(2,1)S(1)}, bf16[256,512]{1,0:T(8,128)(2,1)S(1)}, u32[]{:S(2)}, u32[]{:S(2)}) collective-permute-start(bf16[256,512]{1,0:T(8,128)(2,1)S(1)} %collective-permute-done.2), channel_id=1, source_target_pairs={{0,2},{2,4},{4,6},{6,8},{8,10},{10,12},{12,14},{14,16},{16,18},{18... | collective-permute-start | bytes 786440 | tf_op jit(solution)/shard_map/ppermute | solution.py:22
  31.4 12.1 %collective-permute-start.5 = (bf16[256,512]{1,0:T(8,128)(2,1)S(1)}, bf16[256,512]{1,0:T(8,128)(2,1)S(1)}, u32[]{:S(2)}, u32[]{:S(2)}) collective-permute-start(bf16[256,512]{1,0:T(8,128)(2,1)S(1)} %collective-permute-done.3), channel_id=1, source_target_pairs={{0,30},{2,0},{4,2},{6,4},{8,6},{10,8},{12,10},{14,12},{16,14},{18,... | collective-permute-start | bytes 786440 | tf_op jit(solution)/shard_map/ppermute | solution.py:25
  39.8 10.8 %collective-permute-start.6 = (bf16[256,512]{1,0:T(8,128)(2,1)S(1)}, bf16[256,512]{1,0:T(8,128)(2,1)S(1)}, u32[]{:S(2)}, u32[]{:S(2)}) collective-permute-start(bf16[256,512]{1,0:T(8,128)(2,1)S(1)} %collective-permute-done.4), channel_id=1, source_target_pairs={{0,2},{2,4},{4,6},{6,8},{8,10},{10,12},{12,14},{14,16},{16,18},{18... | collective-permute-start | bytes 786440 | tf_op jit(solution)/shard_map/ppermute | solution.py:22
  42.8 46.1 %copy-start = (bf16[512,4096]{1,0:T(8,128)(2,1)S(1)}, bf16[512,4096]{1,0:T(8,128)(2,1)}, u32[]{:S(2)}) copy-start(bf16[512,4096]{1,0:T(8,128)(2,1)} %param.12) | copy-start | bytes 12582916
  43.5 8.6 %collective-permute-start.7 = (bf16[256,512]{1,0:T(8,128)(2,1)S(1)}, bf16[256,512]{1,0:T(8,128)(2,1)S(1)}, u32[]{:S(2)}, u32[]{:S(2)}) collective-permute-start(bf16[256,512]{1,0:T(8,128)(2,1)S(1)} %collective-permute-done.5), channel_id=1, source_target_pairs={{0,30},{2,0},{4,2},{6,4},{8,6},{10,8},{12,10},{14,12},{16,14},{18,... | collective-permute-start | bytes 786440 | tf_op jit(solution)/shard_map/ppermute | solution.py:25
  50.6 9.2 %collective-permute-start.8 = (bf16[256,512]{1,0:T(8,128)(2,1)S(1)}, bf16[256,512]{1,0:T(8,128)(2,1)S(1)}, u32[]{:S(2)}, u32[]{:S(2)}) collective-permute-start(bf16[256,512]{1,0:T(8,128)(2,1)S(1)} %collective-permute-done.6), channel_id=1, source_target_pairs={{0,2},{2,4},{4,6},{6,8},{8,10},{10,12},{12,14},{14,16},{16,18},{18... | collective-permute-start | bytes 786440 | tf_op jit(solution)/shard_map/ppermute | solution.py:22
  52.1 9.2 %collective-permute-start.9 = (bf16[256,512]{1,0:T(8,128)(2,1)S(1)}, bf16[256,512]{1,0:T(8,128)(2,1)S(1)}, u32[]{:S(2)}, u32[]{:S(2)}) collective-permute-start(bf16[256,512]{1,0:T(8,128)(2,1)S(1)} %collective-permute-done.7), channel_id=1, source_target_pairs={{0,30},{2,0},{4,2},{6,4},{8,6},{10,8},{12,10},{14,12},{16,14},{18,... | collective-permute-start | bytes 786440 | tf_op jit(solution)/shard_map/ppermute | solution.py:25
  59.8 8.7 %collective-permute-start.10 = (bf16[256,512]{1,0:T(8,128)(2,1)S(1)}, bf16[256,512]{1,0:T(8,128)(2,1)S(1)}, u32[]{:S(2)}, u32[]{:S(2)}) collective-permute-start(bf16[256,512]{1,0:T(8,128)(2,1)S(1)} %collective-permute-done.8), channel_id=1, source_target_pairs={{0,2},{2,4},{4,6},{6,8},{8,10},{10,12},{12,14},{14,16},{16,18},{18... | collective-permute-start | bytes 786440 | tf_op jit(solution)/shard_map/ppermute | solution.py:22
  61.2 13.1 %collective-permute-start.11 = (bf16[256,512]{1,0:T(8,128)(2,1)S(1)}, bf16[256,512]{1,0:T(8,128)(2,1)S(1)}, u32[]{:S(2)}, u32[]{:S(2)}) collective-permute-start(bf16[256,512]{1,0:T(8,128)(2,1)S(1)} %collective-permute-done.9), channel_id=1, source_target_pairs={{0,30},{2,0},{4,2},{6,4},{8,6},{10,8},{12,10},{14,12},{16,14},{18,... | collective-permute-start | bytes 786440 | tf_op jit(solution)/shard_map/ppermute | solution.py:25
  68.4 11.2 %collective-permute-start.12 = (bf16[256,512]{1,0:T(8,128)(2,1)S(1)}, bf16[256,512]{1,0:T(8,128)(2,1)S(1)}, u32[]{:S(2)}, u32[]{:S(2)}) collective-permute-start(bf16[256,512]{1,0:T(8,128)(2,1)S(1)} %collective-permute-done.10), channel_id=1, source_target_pairs={{0,2},{2,4},{4,6},{6,8},{8,10},{10,12},{12,14},{14,16},{16,18},{18... | collective-permute-start | bytes 786440 | tf_op jit(solution)/shard_map/ppermute | solution.py:22
  74.3 8.5 %collective-permute-start.13 = (bf16[256,512]{1,0:T(8,128)(2,1)S(1)}, bf16[256,512]{1,0:T(8,128)(2,1)S(1)}, u32[]{:S(2)}, u32[]{:S(2)}) collective-permute-start(bf16[256,512]{1,0:T(8,128)(2,1)S(1)} %collective-permute-done.11), channel_id=1, source_target_pairs={{0,30},{2,0},{4,2},{6,4},{8,6},{10,8},{12,10},{14,12},{16,14},{18,... | collective-permute-start | bytes 786440 | tf_op jit(solution)/shard_map/ppermute | solution.py:25
  79.6 8.5 %collective-permute-start.14 = (bf16[256,512]{1,0:T(8,128)(2,1)S(1)}, bf16[256,512]{1,0:T(8,128)(2,1)S(1)}, u32[]{:S(2)}, u32[]{:S(2)}) collective-permute-start(bf16[256,512]{1,0:T(8,128)(2,1)S(1)} %collective-permute-done.12), channel_id=1, source_target_pairs={{0,2},{2,4},{4,6},{6,8},{8,10},{10,12},{12,14},{14,16},{16,18},{18... | collective-permute-start | bytes 786440 | tf_op jit(solution)/shard_map/ppermute | solution.py:22
  222.8 1.1 copy-start.1
  232.1 18.0 %copy-start.8 = (bf16[512,512]{0,1:T(8,128)(2,1)S(1)}, bf16[512,512]{0,1:T(8,128)(2,1)}, u32[]{:S(2)}) copy-start(bf16[512,512]{0,1:T(8,128)(2,1)} %convolution_convert_fusion) | copy-start | bytes 1572868
  250.1 8.6 %copy-start.3 = (f32[512]{0:T(512)S(1)}, f32[512]{0:T(512)}, u32[]{:S(2)}) copy-start(f32[512]{0:T(512)} %param.19) | copy-start | bytes 6148
  259.2 11.9 %collective-permute-start.15 = (f32[1]{0:T(128)}, f32[1]{0:T(128)}, u32[]{:S(2)}, u32[]{:S(2)}) collective-permute-start(f32[1]{0:T(128)} %slice.35), channel_id=1, source_target_pairs={{2,0},{4,2},{6,4},{8,6},{10,8},{12,10},{14,12},{16,14},{18,16},{20... | collective-permute-start | bytes 20 | tf_op jit(solution)/shard_map/ppermute | solution.py:35
  261.2 7.3 %copy-start.9 = (u32[32]{0:T(128)S(1)}, u32[32]{0:T(128)}, u32[]{:S(2)}) copy-start(u32[32]{0:T(128)} %constant.207) | copy-start | bytes 388
  261.2 9.9 %copy-start.4 = (f32[512]{0:T(512)S(1)}, f32[512]{0:T(512)}, u32[]{:S(2)}) copy-start(f32[512]{0:T(512)} %param.18) | copy-start | bytes 6148
  261.2 129.7 %copy-start.7 = (f32[2048]{0:T(1024)S(1)}, f32[2048]{0:T(1024)}, u32[]{:S(2)}) copy-start(f32[2048]{0:T(1024)} %param.17) | copy-start | bytes 24580
Sparse Core Ops, SparseCore 0:
  10.2 67.2 all-gather.6
  79.6 127.4 all-gather.8
  209.3 125.2 all-gather.12
  336.0 54.8 all-gather.10
